TPU v7x, 32 devices: a whole 2x2x4 slice. The times are simulated.
32 devices in a mesh: conf: 2 (over y), row: 4 (over z), col: 4 (over x, core).
Axes of the slice: x: 2, y: 2, z: 4, core: 2. Of those that a mesh axis runs over, the one named last changes fastest.
Arguments:
- pair_state: bfloat16 [512, 256, 128], P(('conf', 'row'), 'col'), parts along dimension 0, may hold values from -6 to 6
- token_kinds: int32 [512], P('conf'), parts along dimension 0, may hold values from 0 to 31
- first_type_table: bfloat16 [32, 128], replicated, may hold values from -3 to 3
- second_type_table: bfloat16 [32, 128], replicated, may hold values from -3 to 3
- alignment_state: bfloat16 [64, 16384], P(None, ('conf', 'row', 'col')), parts along dimension 1, may hold values from -6 to 6
- alignment_index: int32 [64, 512], P(None, ('conf', 'row', 'col')), parts along dimension 1, may hold values from 0 to 31
- alignment_table: bfloat16 [32, 32], replicated, may hold values from -3 to 3
- first_weight: bfloat16 [32, 32], replicated, may hold values from -1 to 1
- second_weight: bfloat16 [32, 32], replicated, may hold values from -1 to 1
- outer_product_weight: bfloat16 [1024, 128], replicated, may hold values from -1.5 to 1.5
- outer_product_bias: bfloat16 [128], replicated, may hold values from -4 to 4
- pair_block_mask: int32 [32, 16], P(('conf', 'row'), 'col'), parts along dimension 0, may hold values 0 or 1
- transition_gain: float32 [128], replicated, may hold values from 0.25 to 1.75
- transition_gate_up: bfloat16 [128, 1024], replicated, may hold values from -0.5 to 0.5
- transition_down: bfloat16 [512, 128], replicated, may hold values from -0.25 to 0.25
- distance_weight: bfloat16 [128, 64], replicated, may hold values from -0.5 to 0.5
- distance_bias: float32 [64], replicated, may hold values from -4 to 4
Outputs:
- pair_out: bfloat16 [512, 256, 128], P(('conf', 'row'), 'col'), parts along dimension 0
- distogram: bfloat16 [512, 16384], P(('conf', 'row'), 'col'), parts along dimension 0
There are 2 independent parts, one for each index of `conf`. A program takes and returns all parts, laid end to end along the dimension named above; an argument that names none is the same for every part. Nothing has to cross between parts.
All inputs are finite; a program needn't handle non-finite values. No bound on the sum of `pair_block_mask` on one device may be relied on, other than what follows from the above.
Results may differ from a plain program's by a relative error of at most 0.0071.
Values may be sent and summed in bfloat16 or wider, within the bound.
A program may use at most 64 MiB of HBM per device.

v0:
```python
import functools

import jax
import jax.numpy as jnp
from jax import lax
from jax.experimental import pallas as pl
from jax.experimental.pallas import tpu as pltpu
from jax.sharding import PartitionSpec as P

EPSILON = 1e-05
LANES = 128
MESH = pl.DeviceIdType.MESH


def indicator_rows(indices, lookup_table):
    level_values = lookup_table.shape[0]
    onehot = (indices[..., None] == jnp.arange(level_values, dtype=jnp.int32)).astype(jnp.bfloat16)
    return jnp.einsum("...k,kc->...c", onehot, lookup_table, preferred_element_type=jnp.float32)


def kernel(
    ranks,
    depth,
    chunks,
    pair_hbm,
    kinds_ref,
    first_table_ref,
    second_table_ref,
    left_ref,
    right_ref,
    outer_weight_ref,
    outer_bias_ref,
    mask_ref,
    gain_ref,
    gate_up_hbm,
    down_hbm,
    weight_ref,
    dist_bias_ref,
    pair_out_ref,
    dist_out_ref,
    left_all,
    right_all,
    right_float,
    outer_all,
    pair_float,
    right_embed_ref,
    left_embed_ref,
    mirror_send,
    mirror_recv,
    own_part,
    start_ref,
    normed_ref,
    hidden_ref,
    turned_ref,
    left_send_sem,
    left_recv_sem,
    right_send_sem,
    right_recv_sem,
    mirror_send_sem,
    mirror_recv_sem,
    relay_recv,
    relay_recv_sem,
    forward_send_sem,
    dist_weight_wide,
    dist_bias_wide,
    embed_all,
    pair_ref,
    gate_up_ref,
    down_ref,
    load_sem,
):
    conf = lax.axis_index("conf")
    row = lax.axis_index("row")
    col = lax.axis_index("col")
    local_groups, width, span = left_ref.shape
    local_tokens, packed, _ = right_ref.shape
    block = pair_ref.shape[0]
    groups = left_all.shape[0]
    members = span // depth
    pairs = members * block
    per_tile = LANES // depth
    hid = down_ref.shape[0]
    pitch = pair_float.shape[0] // block
    diagonal = row == col

    loads = [
        pltpu.make_async_copy(pair_hbm, pair_ref, load_sem.at[0]),
        pltpu.make_async_copy(gate_up_hbm, gate_up_ref, load_sem.at[1]),
        pltpu.make_async_copy(down_hbm, down_ref, load_sem.at[2]),
    ]
    for load in loads:
        load.start()

    barrier = pltpu.get_barrier_semaphore()
    for step in range(1, ranks):
        pl.semaphore_signal(
            barrier, inc=1, device_id=(conf, row, lax.rem(col + step, ranks)), device_id_type=MESH
        )
    for step in range(ranks):
        source = lax.rem(col + step, ranks)

        @pl.when(jnp.logical_or(jnp.logical_not(diagonal), source != col))
        def _():
            pl.semaphore_signal(
                barrier, inc=1, device_id=(conf, col, source), device_id_type=MESH
            )

    @pl.when(jnp.logical_not(diagonal))
    def _():
        pl.semaphore_signal(barrier, inc=1, device_id=(conf, col, row), device_id_type=MESH)
        pl.semaphore_wait(barrier, 2 * ranks)

    @pl.when(diagonal)
    def _():
        pl.semaphore_wait(barrier, 2 * (ranks - 1))

    def left_copy(peer, slot):
        return pltpu.make_async_remote_copy(
            src_ref=left_ref,
            dst_ref=left_all.at[pl.ds(slot * local_groups, local_groups)],
            send_sem=left_send_sem.at[peer],
            recv_sem=left_recv_sem.at[slot],
            device_id=(conf, row, peer),
            device_id_type=MESH,
        )

    def right_copy(target, slot):
        return pltpu.make_async_remote_copy(
            src_ref=right_ref,
            dst_ref=right_all.at[pl.ds(slot * local_tokens, local_tokens)],
            send_sem=right_send_sem.at[target],
            recv_sem=right_recv_sem.at[slot],
            device_id=(conf, target, row),
            device_id_type=MESH,
        )

    for step in range(ranks):
        target = lax.rem(row + step, ranks)

        @pl.when(jnp.logical_or(jnp.logical_not(diagonal), target != row))
        def _():
            right_copy(target, col).start()

    for step in range(1, ranks):
        left_copy(lax.rem(col + step, ranks), col).start()

    left_all[pl.ds(col * local_groups, local_groups)] = left_ref[...]

    @pl.when(diagonal)
    def _():
        right_all[pl.ds(col * local_tokens, local_tokens)] = right_ref[...]

    tokens = kinds_ref.shape[1]
    levels = lax.broadcasted_iota(jnp.int32, (first_table_ref.shape[0], tokens), 0)
    onehot = (levels == kinds_ref[...]).astype(jnp.float32).astype(jnp.bfloat16)
    for table_ref, embed_ref, place in (
        (first_table_ref, left_embed_ref, row),
        (second_table_ref, right_embed_ref, col),
    ):
        embed_all[...] = lax.dot_general(
            onehot, table_ref[...], (((0,), (0,)), ((), ())), preferred_element_type=jnp.float32
        )
        embed_ref[...] = embed_all[pl.ds(pl.multiple_of(place * block, block), block), :]
    bins = dist_bias_ref.shape[1]
    for place in range(2):
        dist_bias_wide[:, place * bins : (place + 1) * bins] = dist_bias_ref[...]
    dist_weight_wide[...] = jnp.zeros_like(dist_weight_wide)
    depth_of = weight_ref.shape[1]
    for place in range(2):
        dist_weight_wide[
            place * bins : (place + 1) * bins, place * depth_of : (place + 1) * depth_of
        ] = weight_ref[...]

    for step in range(1, ranks):
        peer = lax.rem(col + step, ranks)
        left_copy(peer, peer).wait_recv()
    for step in range(ranks):
        source = lax.rem(col + step, ranks)

        @pl.when(jnp.logical_or(jnp.logical_not(diagonal), source != col))
        def _():
            right_copy(source, source).wait_recv()

    for token in range(0, block, 16):
        part = right_all[token : token + 16]
        right_float[token * packed : (token + 16) * packed, :] = part.reshape(
            16 * packed, LANES
        ).astype(jnp.float32)

    left_rows = left_all[...].reshape(groups * width, span)
    lane = lax.broadcasted_iota(jnp.int32, (block, LANES), 1)
    zero = jnp.zeros((block, LANES), jnp.bfloat16)
    span_tiles = span // LANES

    def outer_step(tile, carry):
        found = right_float[pl.ds(tile, block, stride=packed), :]
        for which in range(per_tile):
            rows = []
            for member in range(members):
                position = member % per_tile
                shift = (position - which) * depth % LANES
                moved = found if shift == 0 else pltpu.roll(found, shift, 1)
                inside = jnp.logical_and(lane >= position * depth, lane < (position + 1) * depth)
                kept = jnp.where(inside, moved, 0.0).astype(jnp.bfloat16)
                rows.append(
                    jnp.concatenate(
                        [kept if t == member // per_tile else zero for t in range(span_tiles)], axis=1
                    )
                )
            spread = jnp.concatenate(rows, axis=0)
            product = lax.dot_general(
                left_rows, spread, (((1,), (1,)), ((), ())), preferred_element_type=jnp.float32
            )
            place = pl.multiple_of((tile * per_tile + which) * width, width)
            outer_all[:, pl.ds(place, width), :] = product.astype(jnp.bfloat16).reshape(
                groups, width, pairs
            )
        return carry

    lax.fori_loop(0, packed, outer_step, 0, unroll=4)

    chips = ranks // 2
    far = (col // 2 == lax.rem(row // 2 + chips // 2, chips)) if chips > 1 else None
    relay = (col // 2 == row // 2) if chips > 1 else None
    relay_col = row // 2 * 2 + lax.rem(col, 2)
    served_col = lax.rem(row // 2 + chips // 2, max(chips, 1)) * 2 + lax.rem(col, 2)
    part_tiles = block // 4 // chunks

    def half_of(chunk, half):
        return pl.ds((chunk * 2 + half) * part_tiles, part_tiles)

    def mirror_copy(chunk, half):
        return pltpu.make_async_remote_copy(
            src_ref=mirror_send.at[half_of(chunk, half)],
            dst_ref=mirror_recv.at[half_of(chunk, half)],
            send_sem=mirror_send_sem.at[half, chunk],
            recv_sem=mirror_recv_sem.at[half, chunk],
            device_id=(conf, col, row),
            device_id_type=MESH,
        )

    def relay_copy(chunk, target):
        return pltpu.make_async_remote_copy(
            src_ref=mirror_send.at[half_of(chunk, 1)],
            dst_ref=relay_recv.at[chunk],
            send_sem=mirror_send_sem.at[1, chunk],
            recv_sem=relay_recv_sem.at[chunk],
            device_id=(conf, row, target),
            device_id_type=MESH,
        )

    def forward_copy(chunk):
        return pltpu.make_async_remote_copy(
            src_ref=relay_recv.at[chunk],
            dst_ref=mirror_recv.at[half_of(chunk, 1)],
            send_sem=forward_send_sem.at[chunk],
            recv_sem=mirror_recv_sem.at[1, chunk],
            device_id=(conf, served_col, row),
            device_id_type=MESH,
        )

    def send_chunk(chunk):
        @pl.when(jnp.logical_not(diagonal))
        def _():
            mirror_copy(chunk, 0).start()

        if chips > 1:

            @pl.when(far)
            def _():
                relay_copy(chunk, relay_col).start()

            @pl.when(jnp.logical_not(jnp.logical_or(diagonal, far)))
            def _():
                mirror_copy(chunk, 1).start()
        else:

            @pl.when(jnp.logical_not(diagonal))
            def _():
                mirror_copy(chunk, 1).start()

    def pass_on(chunk):
        relay_copy(chunk, served_col).wait_recv()
        forward_copy(chunk).start()

    mask_rows, mask_cols = mask_ref.shape
    groups_per_mask = groups // mask_rows
    mask_side = block // mask_cols
    tiles = block // 2 // chunks
    channels = pair_ref.shape[2]

    def project(group):
        return lax.dot_general(
            outer_weight_ref[...], outer_all[group], (((1,), (0,)), ((), ())),
            preferred_element_type=jnp.float32,
        )

    def normalise(group, turned):
        update = turned.T * (1.0 / depth) + outer_bias_ref[...].astype(jnp.float32)
        mask_col = jnp.concatenate(
            [
                jnp.full(
                    (mask_side, channels),
                    mask_ref[group // groups_per_mask, place].astype(jnp.float32),
                    jnp.float32,
                )
                for place in range(mask_cols)
            ],
            axis=0,
        )
        first = pl.multiple_of(group * members, members)
        state = pair_ref[pl.ds(first, members)].astype(jnp.float32)
        left_embed = left_embed_ref[pl.ds(first, members), :]
        start = (
            state
            + left_embed[:, None, :]
            + right_embed_ref[...][None]
            + mask_col[None] * update.reshape(members, block, channels)
        ).reshape(pairs, channels)
        mean = jnp.mean(start, axis=-1, keepdims=True)
        centered = start - mean
        variance = jnp.mean(centered * centered, axis=-1, keepdims=True)
        normed = (centered * lax.rsqrt(variance + EPSILON) * gain_ref[...]).astype(jnp.bfloat16)
        return start, normed

    def expand(normed):
        hidden = []
        for place in range(0, hid, LANES):
            weight = jnp.concatenate(
                [
                    gate_up_ref[:, place : place + LANES],
                    gate_up_ref[:, hid + place : hid + place + LANES],
                ],
                axis=1,
            )
            gate_up = jnp.dot(normed, weight, preferred_element_type=jnp.float32)
            half = 0.5 * gate_up[:, :LANES]
            hidden.append(((half + half * jnp.tanh(half)) * gate_up[:, LANES:]).astype(jnp.bfloat16))
        return jnp.concatenate(hidden, axis=1)

    def contract(start, hidden):
        branch = jnp.dot(hidden, down_ref[...], preferred_element_type=jnp.float32)
        result = (start + branch).astype(jnp.bfloat16)
        shaped = result.reshape(members // 2, 2, block, channels)
        joined = jnp.concatenate([shaped[:, 0], shaped[:, 1]], axis=-1).reshape(
            members // 2 * block, 2 * channels
        )
        part = lax.dot_general(
            joined, dist_weight_wide[...], (((1,), (1,)), ((), ())),
            preferred_element_type=jnp.float32,
        )
        return result, part.astype(jnp.bfloat16).reshape(members // 2, block, LANES)

    for load in loads:
        load.wait()
    last = groups - 1
    begin, normed_first = normalise(0, project(0))
    hidden_ref[...] = expand(normed_first)
    start_ref[0] = begin
    start_ref[1], normed_ref[...] = normalise(1, project(1))
    turned_ref[...] = project(2)

    def group_step(group, carry):
        normed = normed_ref[...]
        turned = turned_ref[...]
        next_turned = project(jnp.minimum(group + 3, last))
        next_hidden = expand(normed)
        result, part = contract(start_ref[0], hidden_ref[...])
        next_start, next_normed = normalise(jnp.minimum(group + 2, last), turned)
        first = pl.multiple_of(group * members, members)
        pair_out_ref[pl.ds(first, members)] = result.reshape(members, block, channels)
        wide = result.astype(jnp.float32)
        for member in range(members):
            pair_float[pl.ds((first + member) * pitch, block), :] = wide[
                member * block : (member + 1) * block
            ]
        mirror_send[pl.ds(group * (members // 2), members // 2)] = part
        turned_ref[...] = next_turned
        hidden_ref[...] = next_hidden
        start_ref[0] = start_ref[1]
        start_ref[1] = next_start
        normed_ref[...] = next_normed
        return carry

    groups_per_chunk = groups // chunks

    def chunk_step(chunk, carry):
        lax.fori_loop(chunk * groups_per_chunk, (chunk + 1) * groups_per_chunk, group_step, 0)

        send_chunk(chunk)
        if chips > 1:

            @pl.when(jnp.logical_and(relay, chunk > 0))
            def _():
                pass_on(chunk - 1)

        return carry

    lax.fori_loop(0, chunks, chunk_step, 0)

    if chips > 1:

        @pl.when(relay)
        def _():
            pass_on(chunks - 1)

    def own_step(tile, carry):
        even = pair_float[pl.ds(2 * tile, block, stride=pitch), :]
        odd = pair_float[pl.ds(2 * tile + 1, block, stride=pitch), :]
        joined = jnp.concatenate([even, odd], axis=1).astype(jnp.bfloat16)
        part = lax.dot_general(
            joined, dist_weight_wide[...], (((1,), (1,)), ((), ())),
            preferred_element_type=jnp.float32,
        )
        own_part[tile] = part.astype(jnp.bfloat16).astype(jnp.float32) + dist_bias_wide[...]
        return carry

    lax.fori_loop(0, block // 2, own_step, 0, unroll=4)

    def finish(tiles_from):
        def step(chunk, carry):
            @pl.when(jnp.logical_not(diagonal))
            def _():
                mirror_copy(chunk, 0).wait_recv()
                mirror_copy(chunk, 1).wait_recv()

            for tile in range(tiles):
                index = chunk * tiles + tile
                total = own_part[index] + tiles_from[index].astype(jnp.float32)
                dist_out_ref[:, pl.ds(pl.multiple_of(index * LANES, LANES), LANES)] = total.astype(
                    jnp.bfloat16
                )
            return carry

        lax.fori_loop(0, chunks, step, 0)

    @pl.when(diagonal)
    def _():
        finish(mirror_send)

    @pl.when(jnp.logical_not(diagonal))
    def _():
        finish(mirror_recv)
        for chunk in range(chunks):
            mirror_copy(chunk, 0).wait_send()
            mirror_copy(chunk, 1).wait_send()

    if chips > 1:

        @pl.when(relay)
        def _():
            for chunk in range(chunks):
                forward_copy(chunk).wait_send()

    for step in range(ranks):
        target = lax.rem(row + step, ranks)

        @pl.when(jnp.logical_or(jnp.logical_not(diagonal), target != row))
        def _():
            right_copy(target, col).wait_send()

    for step in range(1, ranks):
        left_copy(lax.rem(col + step, ranks), col).wait_send()


def local(
    ranks,
    pair_state,
    token_kinds,
    first_type_table,
    second_type_table,
    alignment_state,
    alignment_index,
    alignment_table,
    first_weight,
    second_weight,
    outer_product_weight,
    outer_product_bias,
    pair_block_mask,
    transition_gain,
    transition_gate_up,
    transition_down,
    distance_weight,
    distance_bias,
):
    block = pair_state.shape[0]
    channels = pair_state.shape[2]
    depth, local_tokens = alignment_index.shape
    features = alignment_state.shape[1] // local_tokens
    width = first_weight.shape[1]
    bins = distance_weight.shape[1]
    members = 2 * LANES // depth
    groups = block // members
    local_groups = local_tokens // members
    packed = width * depth // LANES
    chunks = block // 8

    embedded = alignment_state.reshape(depth, local_tokens, features).astype(
        jnp.float32
    ) + indicator_rows(alignment_index, alignment_table)
    embedded = embedded.astype(jnp.bfloat16)
    left = jnp.einsum("snm,mc->ncs", embedded, first_weight, preferred_element_type=jnp.float32)
    right = jnp.einsum("snm,mc->ncs", embedded, second_weight, preferred_element_type=jnp.float32)
    left = (
        left.astype(jnp.bfloat16)
        .reshape(local_groups, members, width, depth)
        .transpose(0, 2, 1, 3)
        .reshape(local_groups, width, members * depth)
    )
    right = right.astype(jnp.bfloat16).reshape(local_tokens, packed, LANES)
    outer_weight = (
        outer_product_weight.reshape(width, width, channels).transpose(2, 1, 0).reshape(channels, -1)
    )
    vmem = pl.BlockSpec(memory_space=pltpu.VMEM)
    smem = pl.BlockSpec(memory_space=pltpu.SMEM)
    hbm = pl.BlockSpec(memory_space=pltpu.HBM)
    pair_out, distogram = pl.pallas_call(
        functools.partial(kernel, ranks, depth, chunks),
        out_shape=(
            jax.ShapeDtypeStruct(pair_state.shape, jnp.bfloat16),
            jax.ShapeDtypeStruct((block, block * bins), jnp.bfloat16),
        ),
        in_specs=[hbm] + [vmem] * 7 + [smem, vmem, hbm, hbm] + [vmem] * 2,
        out_specs=(vmem, vmem),
        scratch_shapes=[
            pltpu.VMEM((groups, width, members * depth), jnp.bfloat16),
            pltpu.VMEM((block, packed, LANES), jnp.bfloat16),
            pltpu.VMEM((block * packed, LANES), jnp.float32),
            pltpu.VMEM((groups, width * width, members * block), jnp.bfloat16),
            pltpu.VMEM((block * (block + 1), channels), jnp.float32),
            pltpu.VMEM((block, channels), jnp.float32),
            pltpu.VMEM((block, channels), jnp.float32),
            pltpu.VMEM((block // 2, block, 2 * bins), jnp.bfloat16),
            pltpu.VMEM((block // 2, block, 2 * bins), jnp.bfloat16),
            pltpu.VMEM((block // 2, block, 2 * bins), jnp.float32),
            pltpu.VMEM((2, members * block, channels), jnp.float32),
            pltpu.VMEM((members * block, channels), jnp.bfloat16),
            pltpu.VMEM((members * block, transition_down.shape[0]), jnp.bfloat16),
            pltpu.VMEM((channels, members * block), jnp.float32),
            pltpu.SemaphoreType.DMA((ranks,)),
            pltpu.SemaphoreType.DMA((ranks,)),
            pltpu.SemaphoreType.DMA((ranks,)),
            pltpu.SemaphoreType.DMA((ranks,)),
            pltpu.SemaphoreType.DMA((2, chunks)),
            pltpu.SemaphoreType.DMA((2, chunks)),
            pltpu.VMEM((chunks, block // 4 // chunks, block, 2 * bins), jnp.bfloat16),
            pltpu.SemaphoreType.DMA((chunks,)),
            pltpu.SemaphoreType.DMA((chunks,)),
            pltpu.VMEM((2 * bins, 2 * channels), jnp.bfloat16),
            pltpu.VMEM((1, 2 * bins), jnp.float32),
            pltpu.VMEM((token_kinds.shape[0], channels), jnp.float32),
            pltpu.VMEM(pair_state.shape, pair_state.dtype),
            pltpu.VMEM(transition_gate_up.shape, transition_gate_up.dtype),
            pltpu.VMEM(transition_down.shape, transition_down.dtype),
            pltpu.SemaphoreType.DMA((3,)),
        ],
        compiler_params=pltpu.CompilerParams(
            collective_id=0, has_side_effects=True, vmem_limit_bytes=48 * 1024 * 1024
        ),
    )(
        pair_state,
        token_kinds[None],
        first_type_table,
        second_type_table,
        left,
        right,
        outer_weight,
        outer_product_bias[None],
        pair_block_mask,
        transition_gain[None],
        transition_gate_up,
        transition_down,
        distance_weight.T,
        distance_bias[None],
    )
    return pair_out, distogram


def solution(mesh):
    in_specs = (
        P(("conf", "row"), "col", None),
        P("conf"),
        P(),
        P(),
        P(None, ("conf", "row", "col")),
        P(None, ("conf", "row", "col")),
        P(),
        P(),
        P(),
        P(),
        P(),
        P(("conf", "row"), "col"),
        P(),
        P(),
        P(),
        P(),
        P(),
    )
    out_specs = (P(("conf", "row"), "col", None), P(("conf", "row"), "col"))
    return jax.shard_map(
        functools.partial(local, mesh.shape["col"]),
        mesh=mesh,
        in_specs=in_specs,
        out_specs=out_specs,
        check_vma=False,
    )
```

profile of v0, /device:TPU:7, one launch (start us, length us, event | category | flops | bytes accessed | tf_op | source)
XLA Modules:
  0.0 40.7 jit_solution(3120457448976463841)
XLA Ops:
  0.6 0.0 copy-start
  0.7 0.9 %copy.31 = f32[64,512]{0,1:T(8,128)S(1)} copy(bf16[64,512]{1,0:T(8,128)(2,1)} %param.21) | data formatting | bytes 196608 | tf_op jit(solution)/shard_map/convert_element_type | solution.py:498
  1.6 0.0 copy-start.14
  1.6 0.2 fusion
  1.9 0.5 %copy-done.14 = bf16[32,32]{1,0:T(8,128)(2,1)S(1)} copy-done((bf16[32,32]{1,0:T(8,128)(2,1)S(1)}, bf16[32,32]{1,0:T(8,128)(2,1)}, u32[]{:S(2)}) %copy-start.14) | copy-done | bytes 2072
  2.3 0.2 fusion.1
  2.6 0.0 copy-start.1
  2.6 0.1 reshape.25.right_ref
  2.7 0.3 copy-done.15
  3.0 0.2 convolution_convert_fusion.1
  3.3 0.1 copy.45
  3.3 0.1 reshape.24.left_ref
  3.5 0.1 copy.36
  3.6 0.0 copy-start.3
  3.6 0.0 copy-start.4
  3.7 0.0 copy-start.7
  3.7 0.0 copy-start.8
  3.7 0.0 copy-start.11
  3.7 0.1 copy.37.outer_weight_ref
  3.9 0.7 %copy-done.2 = bf16[128,1024]{1,0:T(8,128)(2,1)S(1)} copy-done((bf16[128,1024]{1,0:T(8,128)(2,1)S(1)}, bf16[128,1024]{1,0:T(8,128)(2,1)}, u32[]{:S(2)}) %copy-start.2) | copy-done | bytes 262168
  4.6 0.0 copy-done.3
  4.7 34.2 %shard_map.176 = (bf16[64,64,128]{2,1,0:T(8,128)(2,1)S(1)}, bf16[64,4096]{1,0:T(8,128)(2,1)S(1)}) custom-call(bf16[64,64,128]{2,1,0:T(8,128)(2,1)S(1)} %copy-done.1, s32[1,256]{1,0:T(1,128)S(1)} %bitcast.30, bf16[32,128]{1,0:T(8,128)(2,1)S(1)} %copy-done.5, bf16[32,128]{1,0:T(8,128)(2,1)S(1)} %copy-done.6, bf16[4,32,256]{2,1,0:T(8,128)(2,1)S(1)} %reshape.24.left_ref, ...), custom_call_target="tpu_custom_call" | custom-call | tf_op jit(solution)/shard_map/pallas_call | solution.py:517
  38.9 1.0 %copy.48 = bf16[64,64,128]{2,1,0:T(8,128)(2,1)} copy(bf16[64,64,128]{2,1,0:T(8,128)(2,1)S(1)} %get-tuple-element.4) | data formatting | bytes 2097152
  39.9 0.8 %copy.49 = bf16[64,4096]{1,0:T(8,128)(2,1)} copy(bf16[64,4096]{1,0:T(8,128)(2,1)S(1)} %get-tuple-element.5) | data formatting | bytes 1048576
  (20 shorter events, 0.1 us)
Async XLA Ops:
  0.6 1.0 %copy-start = (bf16[32,32]{1,0:T(8,128)(2,1)S(1)}, bf16[32,32]{1,0:T(8,128)(2,1)}, u32[]{:S(2)}) copy-start(bf16[32,32]{1,0:T(8,128)(2,1)} %param.23) | copy-start | bytes 6148
  0.6 1.0 %copy-start.13 = (s32[64,16]{0,1:T(8,128)S(1)}, s32[64,16]{0,1:T(8,128)}, u32[]{:S(2)}) copy-start(s32[64,16]{0,1:T(8,128)} %param.22) | copy-start | bytes 12292
  1.6 0.7 %copy-start.14 = (bf16[32,32]{1,0:T(8,128)(2,1)S(1)}, bf16[32,32]{1,0:T(8,128)(2,1)}, u32[]{:S(2)}) copy-start(bf16[32,32]{1,0:T(8,128)(2,1)} %param.25) | copy-start | bytes 6148
  2.3 0.7 %copy-start.15 = (bf16[32,32]{1,0:T(8,128)(2,1)S(1)}, bf16[32,32]{1,0:T(8,128)(2,1)}, u32[]{:S(2)}) copy-start(bf16[32,32]{1,0:T(8,128)(2,1)} %param.24) | copy-start | bytes 6148
  2.3 1.2 %copy-start.12 = (bf16[1024,128]{1,0:T(8,128)(2,1)S(1)}, bf16[1024,128]{1,0:T(8,128)(2,1)}, u32[]{:S(2)}) copy-start(bf16[1024,128]{1,0:T(8,128)(2,1)} %param.26) | copy-start | bytes 786436
  2.6 1.3 %copy-start.1 = (bf16[64,64,128]{2,1,0:T(8,128)(2,1)S(1)}, bf16[64,64,128]{2,1,0:T(8,128)(2,1)}, u32[]{:S(2)}) copy-start(bf16[64,64,128]{2,1,0:T(8,128)(2,1)} %pair_hbm.1) | copy-start | bytes 3145732
  3.6 1.0 %copy-start.2 = (bf16[128,1024]{1,0:T(8,128)(2,1)S(1)}, bf16[128,1024]{1,0:T(8,128)(2,1)}, u32[]{:S(2)}) copy-start(bf16[128,1024]{1,0:T(8,128)(2,1)} %gate_up_hbm.1) | copy-start | bytes 786436
  3.6 1.0 %copy-start.3 = (bf16[512,128]{1,0:T(8,128)(2,1)S(1)}, bf16[512,128]{1,0:T(8,128)(2,1)}, u32[]{:S(2)}) copy-start(bf16[512,128]{1,0:T(8,128)(2,1)} %down_hbm.1) | copy-start | bytes 393220
  3.6 1.0 %copy-start.4 = (bf16[128,64]{0,1:T(8,128)(2,1)S(1)}, bf16[128,64]{0,1:T(8,128)(2,1)}, u32[]{:S(2)}) copy-start(bf16[128,64]{0,1:T(8,128)(2,1)} %param.32) | copy-start | bytes 49156
  3.6 1.0 %copy-start.5 = (bf16[32,128]{1,0:T(8,128)(2,1)S(1)}, bf16[32,128]{1,0:T(8,128)(2,1)}, u32[]{:S(2)}) copy-start(bf16[32,128]{1,0:T(8,128)(2,1)} %first_table_ref.1) | copy-start | bytes 24580
  3.7 1.0 %copy-start.6 = (bf16[32,128]{1,0:T(8,128)(2,1)S(1)}, bf16[32,128]{1,0:T(8,128)(2,1)}, u32[]{:S(2)}) copy-start(bf16[32,128]{1,0:T(8,128)(2,1)} %second_table_ref.1) | copy-start | bytes 24580
  3.7 1.0 %copy-start.7 = (s32[4,4]{1,0:T(4,128)S(1)}, s32[4,4]{1,0:T(4,128)}, u32[]{:S(2)}) copy-start(s32[4,4]{1,0:T(4,128)} %mask_ref.1) | copy-start | bytes 196
  3.7 1.0 %copy-start.8 = (s32[256]{0:T(256)S(1)}, s32[256]{0:T(256)}, u32[]{:S(2)}) copy-start(s32[256]{0:T(256)} %param.18) | copy-start | bytes 3076
  3.7 1.0 %copy-start.9 = (bf16[128]{0:T(256)(128)(2,1)S(1)}, bf16[128]{0:T(256)(128)(2,1)}, u32[]{:S(2)}) copy-start(bf16[128]{0:T(256)(128)(2,1)} %param.27) | copy-start | bytes 772
  3.7 1.0 %copy-start.10 = (f32[128]{0:T(128)S(1)}, f32[128]{0:T(128)}, u32[]{:S(2)}) copy-start(f32[128]{0:T(128)} %param.29) | copy-start | bytes 1540
  3.7 1.0 %copy-start.11 = (f32[64]{0:T(128)S(1)}, f32[64]{0:T(128)}, u32[]{:S(2)}) copy-start(f32[64]{0:T(128)} %param.33) | copy-start | bytes 772
where the time goes:
time: 41 us; the launch traced here: 40.7 us
  Pallas kernels  34.2 us (83%)
  local copies, waits for them, and re-layouts  4.92 us (12%)
  between operations  0.88 us (2%)
  matrix products  0.66 us (2%)
    pallas_call x1, Pallas kernels, local(): pl.pallas_call(functools.partial(kernel, ranks, depth, chunks), out_shape...  34.2 us
    unnamed x34, local copies, waits for them, and re-layouts  3.39 us
    convert_element_type x1, local copies, waits for them, and re-layouts, local(): alignment_state.reshape(depth, local_tokens, features).astype(jnp.float32)  0.95 us

commit v1 on v0

--- a/solution.py
+++ b/solution.py
@@ -12,10 +12,91 @@
 MESH = pl.DeviceIdType.MESH
 
 
-def indicator_rows(indices, lookup_table):
-    level_values = lookup_table.shape[0]
-    onehot = (indices[..., None] == jnp.arange(level_values, dtype=jnp.int32)).astype(jnp.bfloat16)
-    return jnp.einsum("...k,kc->...c", onehot, lookup_table, preferred_element_type=jnp.float32)
+def project_tokens(
+    depth, state_ref, index_ref, table_ref, first_weight_ref, second_weight_ref, left_ref, right_ref
+):
+    levels, features = table_ref.shape
+    width = first_weight_ref.shape[1]
+    tokens = index_ref.shape[0]
+    per_tile = LANES // features
+    tiles = tokens // per_tile
+    packed = LANES // depth
+
+    def iota(shape, axis):
+        return lax.broadcasted_iota(jnp.int32, shape, axis)
+
+    def indicator(inside):
+        return inside.astype(jnp.float32).astype(jnp.bfloat16)
+
+    def dot(left, right, dims):
+        return lax.dot_general(left, right, (dims, ((), ())), preferred_element_type=jnp.float32)
+
+    repeat = indicator(iota((LANES, features), 0) % features == iota((LANES, features), 1))
+    wide = per_tile * levels
+    repeat_levels = indicator(iota((wide, levels), 0) % levels == iota((wide, levels), 1))
+    table_rows = dot(repeat_levels, table_ref[...], ((1,), (0,))).astype(jnp.bfloat16)
+    table_wide = jnp.where(
+        iota((wide, LANES), 0) // levels == iota((wide, LANES), 1) // features,
+        dot(table_rows, repeat, ((1,), (1,))),
+        0.0,
+    ).astype(jnp.bfloat16)
+    first_wide = dot(first_weight_ref[...], repeat, ((0,), (1,))).astype(jnp.bfloat16)
+    second_wide = dot(second_weight_ref[...], repeat, ((0,), (1,))).astype(jnp.bfloat16)
+
+    rows = width // packed * tokens
+    token_of = iota((rows, LANES), 0) % tokens
+    slot_of = iota((rows, LANES), 1) // features
+    picks = []
+    for position in range(packed):
+        pick = indicator(
+            iota((rows, width), 0) // tokens * packed + position == iota((rows, width), 1)
+        )
+        spread = dot(pick, second_wide, ((1,), (0,)))
+        for tile in range(tiles):
+            picks.append(
+                jnp.where(token_of == tile * per_tile + slot_of, spread, 0.0).astype(jnp.bfloat16)
+            )
+
+    spread_index = indicator(
+        iota((tokens, tokens * levels), 1) // levels == iota((tokens, tokens * levels), 0)
+    )
+    index_wide = dot(
+        index_ref[...].astype(jnp.float32).astype(jnp.bfloat16), spread_index, ((0,), (0,))
+    )
+    level_of = (iota((depth, tokens * levels), 1) % levels).astype(jnp.float32)
+    onehot = indicator(index_wide == level_of)
+    lane_slot = iota((depth, LANES), 1) // features
+    embedded = []
+    for tile in range(tiles):
+        looked = dot(onehot[:, tile * wide : (tile + 1) * wide], table_wide, ((1,), (0,)))
+        state = state_ref[:, tile * LANES : (tile + 1) * LANES].astype(jnp.float32)
+        value = (state + looked).astype(jnp.bfloat16).astype(jnp.float32)
+        embedded.append(value.astype(jnp.bfloat16))
+        stack = jnp.concatenate(
+            [
+                jnp.where(lane_slot == slot, value, 0.0).astype(jnp.bfloat16)
+                for slot in range(per_tile)
+            ],
+            axis=0,
+        )
+        left_ref[tile] = dot(first_wide, stack, ((1,), (1,))).astype(jnp.bfloat16)
+
+    blank = jnp.zeros((depth, LANES), jnp.bfloat16)
+    parts = []
+    for position in range(packed):
+        for tile in range(tiles):
+            parts.append(
+                jnp.concatenate(
+                    [embedded[tile] if place == position else blank for place in range(packed)], axis=0
+                )
+            )
+    right = dot(
+        jnp.concatenate(picks, axis=1), jnp.concatenate(parts, axis=1), ((1,), (1,))
+    )
+    for place in range(width // packed):
+        right_ref[:, place * LANES : (place + 1) * LANES] = right[
+            place * tokens : (place + 1) * tokens
+        ].astype(jnp.bfloat16)
 
 
 def kernel(
@@ -23,25 +104,32 @@
     depth,
     chunks,
     pair_hbm,
-    kinds_ref,
-    first_table_ref,
-    second_table_ref,
+    kinds_hbm,
+    first_table_hbm,
+    second_table_hbm,
+    state_hbm,
+    index_hbm,
+    align_table_hbm,
+    first_weight_hbm,
+    second_weight_hbm,
+    outer_weight_hbm,
+    outer_bias_hbm,
+    mask_hbm,
+    gain_hbm,
+    gate_up_hbm,
+    down_hbm,
+    weight_hbm,
+    dist_bias_hbm,
+    pair_out_ref,
+    dist_out_ref,
     left_ref,
     right_ref,
-    outer_weight_ref,
-    outer_bias_ref,
-    mask_ref,
-    gain_ref,
-    gate_up_hbm,
-    down_hbm,
-    weight_ref,
-    dist_bias_ref,
-    pair_out_ref,
-    dist_out_ref,
     left_all,
     right_all,
-    right_float,
-    outer_all,
+    outer_ref,
+    outer_weight_raw,
+    outer_weight_float,
+    outer_weight_ref,
     pair_float,
     right_embed_ref,
     left_embed_ref,
@@ -50,8 +138,6 @@
     own_part,
     start_ref,
     normed_ref,
-    hidden_ref,
-    turned_ref,
     left_send_sem,
     left_recv_sem,
     right_send_sem,
@@ -65,31 +151,64 @@
     dist_bias_wide,
     embed_all,
     pair_ref,
+    kinds_ref,
+    first_table_ref,
+    second_table_ref,
+    state_ref,
+    index_ref,
+    align_table_ref,
+    first_weight_ref,
+    second_weight_ref,
+    outer_bias_ref,
+    mask_ref,
+    gain_ref,
     gate_up_ref,
     down_ref,
+    weight_ref,
+    dist_bias_ref,
     load_sem,
 ):
     conf = lax.axis_index("conf")
     row = lax.axis_index("row")
     col = lax.axis_index("col")
     local_groups, width, span = left_ref.shape
-    local_tokens, packed, _ = right_ref.shape
+    local_tokens = right_ref.shape[0]
     block = pair_ref.shape[0]
     groups = left_all.shape[0]
     members = span // depth
     pairs = members * block
-    per_tile = LANES // depth
     hid = down_ref.shape[0]
     pitch = pair_float.shape[0] // block
     diagonal = row == col
 
-    loads = [
-        pltpu.make_async_copy(pair_hbm, pair_ref, load_sem.at[0]),
-        pltpu.make_async_copy(gate_up_hbm, gate_up_ref, load_sem.at[1]),
-        pltpu.make_async_copy(down_hbm, down_ref, load_sem.at[2]),
+    def load(place, source, target):
+        return pltpu.make_async_copy(source, target, load_sem.at[place])
+
+    early = [
+        load(0, index_hbm, index_ref),
+        load(1, state_hbm, state_ref),
+        load(2, align_table_hbm, align_table_ref),
+        load(3, first_weight_hbm, first_weight_ref),
+        load(4, second_weight_hbm, second_weight_ref),
     ]
-    for load in loads:
-        load.start()
+    later = [
+        load(5, kinds_hbm, kinds_ref),
+        load(6, first_table_hbm, first_table_ref),
+        load(7, second_table_hbm, second_table_ref),
+        load(8, weight_hbm, weight_ref),
+        load(9, dist_bias_hbm, dist_bias_ref),
+        load(10, outer_weight_hbm, outer_weight_raw),
+    ]
+    last_loads = [
+        load(11, pair_hbm, pair_ref),
+        load(12, outer_bias_hbm, outer_bias_ref),
+        load(13, mask_hbm, mask_ref),
+        load(14, gain_hbm, gain_ref),
+        load(15, gate_up_hbm, gate_up_ref),
+        load(16, down_hbm, down_ref),
+    ]
+    for copy in early:
+        copy.start()
 
     barrier = pltpu.get_barrier_semaphore()
     for step in range(1, ranks):
@@ -108,6 +227,17 @@
     @pl.when(jnp.logical_not(diagonal))
     def _():
         pl.semaphore_signal(barrier, inc=1, device_id=(conf, col, row), device_id_type=MESH)
+
+    for copy in later + last_loads:
+        copy.start()
+    for copy in early:
+        copy.wait()
+    project_tokens(
+        depth, state_ref, index_ref, align_table_ref, first_weight_ref, second_weight_ref, left_ref, right_ref
+    )
+
+    @pl.when(jnp.logical_not(diagonal))
+    def _():
         pl.semaphore_wait(barrier, 2 * ranks)
 
     @pl.when(diagonal)
@@ -127,7 +257,7 @@
     def right_copy(target, slot):
         return pltpu.make_async_remote_copy(
             src_ref=right_ref,
-            dst_ref=right_all.at[pl.ds(slot * local_tokens, local_tokens)],
+            dst_ref=right_all.at[slot],
             send_sem=right_send_sem.at[target],
             recv_sem=right_recv_sem.at[slot],
             device_id=(conf, target, row),
@@ -148,8 +278,10 @@
 
     @pl.when(diagonal)
     def _():
-        right_all[pl.ds(col * local_tokens, local_tokens)] = right_ref[...]
-
+        right_all[col] = right_ref[...]
+
+    for copy in later:
+        copy.wait()
     tokens = kinds_ref.shape[1]
     levels = lax.broadcasted_iota(jnp.int32, (first_table_ref.shape[0], tokens), 0)
     onehot = (levels == kinds_ref[...]).astype(jnp.float32).astype(jnp.bfloat16)
@@ -171,6 +303,14 @@
             place * bins : (place + 1) * bins, place * depth_of : (place + 1) * depth_of
         ] = weight_ref[...]
 
+    outer_weight_float[...] = outer_weight_raw[...].astype(jnp.float32)
+    for index in range(width):
+        outer_weight_ref[index * width : (index + 1) * width, :] = outer_weight_float[
+            pl.ds(index, width, stride=width), :
+        ].astype(jnp.bfloat16)
+    for copy in last_loads:
+        copy.wait()
+
     for step in range(1, ranks):
         peer = lax.rem(col + step, ranks)
         left_copy(peer, peer).wait_recv()
@@ -181,43 +321,58 @@
         def _():
             right_copy(source, source).wait_recv()
 
-    for token in range(0, block, 16):
-        part = right_all[token : token + 16]
-        right_float[token * packed : (token + 16) * packed, :] = part.reshape(
-            16 * packed, LANES
-        ).astype(jnp.float32)
-
-    left_rows = left_all[...].reshape(groups * width, span)
-    lane = lax.broadcasted_iota(jnp.int32, (block, LANES), 1)
-    zero = jnp.zeros((block, LANES), jnp.bfloat16)
+    lane = lax.broadcasted_iota(jnp.int32, (width, LANES), 1)
+    packed = LANES // depth
     span_tiles = span // LANES
-
-    def outer_step(tile, carry):
-        found = right_float[pl.ds(tile, block, stride=packed), :]
-        for which in range(per_tile):
-            rows = []
-            for member in range(members):
-                position = member % per_tile
-                shift = (position - which) * depth % LANES
-                moved = found if shift == 0 else pltpu.roll(found, shift, 1)
+    zero = jnp.zeros((width, LANES), jnp.bfloat16)
+    spans = right_ref.shape[1] // span
+
+    def right_rows(place):
+        found = [
+            right_all[source, :, place * span : (place + 1) * span] for source in range(ranks)
+        ]
+        if local_tokens % 16 == 0:
+            return jnp.concatenate(found, axis=0)
+        return jnp.concatenate([part.astype(jnp.float32) for part in found], axis=0).astype(jnp.bfloat16)
+
+    def outer(group):
+        found = [
+            left_all[group, :, tile * LANES : (tile + 1) * LANES].astype(jnp.float32)
+            for tile in range(span_tiles)
+        ]
+        spread = []
+        for member in range(members):
+            kept = []
+            for position in range(packed):
+                shift = (position - member % packed) * depth % LANES
+                moved = found[member // packed]
+                moved = moved if shift == 0 else pltpu.roll(moved, shift, 1)
                 inside = jnp.logical_and(lane >= position * depth, lane < (position + 1) * depth)
-                kept = jnp.where(inside, moved, 0.0).astype(jnp.bfloat16)
-                rows.append(
+                kept.append(jnp.where(inside, moved, 0.0).astype(jnp.bfloat16))
+            for place in range(members):
+                spread.append(
                     jnp.concatenate(
-                        [kept if t == member // per_tile else zero for t in range(span_tiles)], axis=1
+                        [kept[place % packed] if t == place // packed else zero for t in range(span_tiles)],
+                        axis=1,
                     )
                 )
-            spread = jnp.concatenate(rows, axis=0)
+        rows = jnp.concatenate([right_rows(place) for place in range(spans)], axis=0)
+        wide = members * width
+        for first in range(0, members, 2):
             product = lax.dot_general(
-                left_rows, spread, (((1,), (1,)), ((), ())), preferred_element_type=jnp.float32
-            )
-            place = pl.multiple_of((tile * per_tile + which) * width, width)
-            outer_all[:, pl.ds(place, width), :] = product.astype(jnp.bfloat16).reshape(
-                groups, width, pairs
-            )
-        return carry
-
-    lax.fori_loop(0, packed, outer_step, 0, unroll=4)
+                rows,
+                jnp.concatenate(spread[first * members : (first + 2) * members], axis=0),
+                (((1,), (1,)), ((), ())),
+                preferred_element_type=jnp.float32,
+            ).astype(jnp.bfloat16)
+            for member in range(2):
+                for place in range(spans):
+                    outer_ref[
+                        (first + member) * block : (first + member + 1) * block,
+                        place * wide : (place + 1) * wide,
+                    ] = product[
+                        place * block : (place + 1) * block, member * wide : (member + 1) * wide
+                    ]
 
     chips = ranks // 2
     far = (col // 2 == lax.rem(row // 2 + chips // 2, chips)) if chips > 1 else None
@@ -289,14 +444,11 @@
     tiles = block // 2 // chunks
     channels = pair_ref.shape[2]
 
-    def project(group):
-        return lax.dot_general(
-            outer_weight_ref[...], outer_all[group], (((1,), (0,)), ((), ())),
-            preferred_element_type=jnp.float32,
-        )
-
-    def normalise(group, turned):
-        update = turned.T * (1.0 / depth) + outer_bias_ref[...].astype(jnp.float32)
+    def project():
+        return jnp.dot(outer_ref[...], outer_weight_ref[...], preferred_element_type=jnp.float32)
+
+    def normalise(group, summed):
+        update = summed * (1.0 / depth) + outer_bias_ref[...].astype(jnp.float32)
         mask_col = jnp.concatenate(
             [
                 jnp.full(
@@ -351,22 +503,18 @@
         )
         return result, part.astype(jnp.bfloat16).reshape(members // 2, block, LANES)
 
-    for load in loads:
-        load.wait()
     last = groups - 1
-    begin, normed_first = normalise(0, project(0))
-    hidden_ref[...] = expand(normed_first)
-    start_ref[0] = begin
-    start_ref[1], normed_ref[...] = normalise(1, project(1))
-    turned_ref[...] = project(2)
+    outer(0)
+    start_ref[...], normed_ref[...] = normalise(0, project())
+    outer(1)
 
     def group_step(group, carry):
-        normed = normed_ref[...]
-        turned = turned_ref[...]
-        next_turned = project(jnp.minimum(group + 3, last))
-        next_hidden = expand(normed)
-        result, part = contract(start_ref[0], hidden_ref[...])
-        next_start, next_normed = normalise(jnp.minimum(group + 2, last), turned)
+        start = start_ref[...]
+        hidden = expand(normed_ref[...])
+        summed = project()
+        result, part = contract(start, hidden)
+        next_start, next_normed = normalise(jnp.minimum(group + 1, last), summed)
+        outer(jnp.minimum(group + 2, last))
         first = pl.multiple_of(group * members, members)
         pair_out_ref[pl.ds(first, members)] = result.reshape(members, block, channels)
         wide = result.astype(jnp.float32)
@@ -375,10 +523,7 @@
                 member * block : (member + 1) * block
             ]
         mirror_send[pl.ds(group * (members // 2), members // 2)] = part
-        turned_ref[...] = next_turned
-        hidden_ref[...] = next_hidden
-        start_ref[0] = start_ref[1]
-        start_ref[1] = next_start
+        start_ref[...] = next_start
         normed_ref[...] = next_normed
         return carry
 
@@ -492,27 +637,9 @@
     members = 2 * LANES // depth
     groups = block // members
     local_groups = local_tokens // members
-    packed = width * depth // LANES
     chunks = block // 8
 
-    embedded = alignment_state.reshape(depth, local_tokens, features).astype(
-        jnp.float32
-    ) + indicator_rows(alignment_index, alignment_table)
-    embedded = embedded.astype(jnp.bfloat16)
-    left = jnp.einsum("snm,mc->ncs", embedded, first_weight, preferred_element_type=jnp.float32)
-    right = jnp.einsum("snm,mc->ncs", embedded, second_weight, preferred_element_type=jnp.float32)
-    left = (
-        left.astype(jnp.bfloat16)
-        .reshape(local_groups, members, width, depth)
-        .transpose(0, 2, 1, 3)
-        .reshape(local_groups, width, members * depth)
-    )
-    right = right.astype(jnp.bfloat16).reshape(local_tokens, packed, LANES)
-    outer_weight = (
-        outer_product_weight.reshape(width, width, channels).transpose(2, 1, 0).reshape(channels, -1)
-    )
     vmem = pl.BlockSpec(memory_space=pltpu.VMEM)
-    smem = pl.BlockSpec(memory_space=pltpu.SMEM)
     hbm = pl.BlockSpec(memory_space=pltpu.HBM)
     pair_out, distogram = pl.pallas_call(
         functools.partial(kernel, ranks, depth, chunks),
@@ -520,23 +647,25 @@
             jax.ShapeDtypeStruct(pair_state.shape, jnp.bfloat16),
             jax.ShapeDtypeStruct((block, block * bins), jnp.bfloat16),
         ),
-        in_specs=[hbm] + [vmem] * 7 + [smem, vmem, hbm, hbm] + [vmem] * 2,
+        in_specs=[hbm] * 17,
         out_specs=(vmem, vmem),
         scratch_shapes=[
+            pltpu.VMEM((local_groups, width, members * depth), jnp.bfloat16),
+            pltpu.VMEM((local_tokens, width * depth), jnp.bfloat16),
             pltpu.VMEM((groups, width, members * depth), jnp.bfloat16),
-            pltpu.VMEM((block, packed, LANES), jnp.bfloat16),
-            pltpu.VMEM((block * packed, LANES), jnp.float32),
-            pltpu.VMEM((groups, width * width, members * block), jnp.bfloat16),
+            pltpu.VMEM((ranks, local_tokens, width * depth), jnp.bfloat16),
+            pltpu.VMEM((members * block, width * width), jnp.bfloat16),
+            pltpu.VMEM(outer_product_weight.shape, jnp.bfloat16),
+            pltpu.VMEM(outer_product_weight.shape, jnp.float32),
+            pltpu.VMEM(outer_product_weight.shape, jnp.bfloat16),
             pltpu.VMEM((block * (block + 1), channels), jnp.float32),
             pltpu.VMEM((block, channels), jnp.float32),
             pltpu.VMEM((block, channels), jnp.float32),
             pltpu.VMEM((block // 2, block, 2 * bins), jnp.bfloat16),
             pltpu.VMEM((block // 2, block, 2 * bins), jnp.bfloat16),
             pltpu.VMEM((block // 2, block, 2 * bins), jnp.float32),
-            pltpu.VMEM((2, members * block, channels), jnp.float32),
+            pltpu.VMEM((members * block, channels), jnp.float32),
             pltpu.VMEM((members * block, channels), jnp.bfloat16),
-            pltpu.VMEM((members * block, transition_down.shape[0]), jnp.bfloat16),
-            pltpu.VMEM((channels, members * block), jnp.float32),
             pltpu.SemaphoreType.DMA((ranks,)),
             pltpu.SemaphoreType.DMA((ranks,)),
             pltpu.SemaphoreType.DMA((ranks,)),
@@ -550,21 +679,37 @@
             pltpu.VMEM((1, 2 * bins), jnp.float32),
             pltpu.VMEM((token_kinds.shape[0], channels), jnp.float32),
             pltpu.VMEM(pair_state.shape, pair_state.dtype),
+            pltpu.VMEM((1, token_kinds.shape[0]), jnp.int32),
+            pltpu.VMEM(first_type_table.shape, jnp.bfloat16),
+            pltpu.VMEM(second_type_table.shape, jnp.bfloat16),
+            pltpu.VMEM(alignment_state.shape, jnp.bfloat16),
+            pltpu.VMEM((local_tokens, depth), jnp.int32),
+            pltpu.VMEM(alignment_table.shape, jnp.bfloat16),
+            pltpu.VMEM(first_weight.shape, jnp.bfloat16),
+            pltpu.VMEM(second_weight.shape, jnp.bfloat16),
+            pltpu.VMEM((1, channels), jnp.bfloat16),
+            pltpu.SMEM(pair_block_mask.shape, jnp.int32),
+            pltpu.VMEM((1, channels), jnp.float32),
             pltpu.VMEM(transition_gate_up.shape, transition_gate_up.dtype),
             pltpu.VMEM(transition_down.shape, transition_down.dtype),
-            pltpu.SemaphoreType.DMA((3,)),
+            pltpu.VMEM((bins, channels), jnp.bfloat16),
+            pltpu.VMEM((1, bins), jnp.float32),
+            pltpu.SemaphoreType.DMA((17,)),
         ],
         compiler_params=pltpu.CompilerParams(
-            collective_id=0, has_side_effects=True, vmem_limit_bytes=48 * 1024 * 1024
+            collective_id=0, has_side_effects=True, vmem_limit_bytes=60 * 1024 * 1024
         ),
     )(
         pair_state,
         token_kinds[None],
         first_type_table,
         second_type_table,
-        left,
-        right,
-        outer_weight,
+        alignment_state,
+        alignment_index.T,
+        alignment_table,
+        first_weight,
+        second_weight,
+        outer_product_weight,
         outer_product_bias[None],
         pair_block_mask,
         transition_gain[None],

time: 41 us -> 38.2 us (0.932)
  local copies, waits for them, and re-layouts: 4.92 us -> 3.12 us
  matrix products: 0.66 us -> 0 us
    convert_element_type x1 -> x0, local copies, waits for them, and re-layouts: 0.95 us -> none  [local(): alignment_state.reshape(depth, local_tokens, features).astype(jnp.float32)]
    dot_general x3 -> x0, matrix products: 0.66 us -> none  [the longest x1 0.22 us: indicator_rows(): jnp.einsum('...k,kc->...c', onehot, lookup_table, preferred_element_type=...]
    reshape x4 -> x0, local copies, waits for them, and re-layouts: 0.48 us -> none  [the longest x2 0.22 us: local(): left = left.astype(jnp.bfloat16).reshape(local_groups, members, width, de...]
    unnamed x34 -> x4, local copies, waits for them, and re-layouts: 3.39 us -> 3.12 us
where the time goes in v1:
time: 38.2 us; the launch traced here: 38 us
  Pallas kernels  34.2 us (90%)
  local copies, waits for them, and re-layouts  3.12 us (8%)
  between operations  0.65 us (2%)
    pallas_call x1, Pallas kernels, local(): pl.pallas_call(functools.partial(kernel, ranks, depth, chunks), out_shape...  34.2 us
    unnamed x4, local copies, waits for them, and re-layouts  3.12 us

profile of v1, /device:TPU:7, one launch (start us, length us, event | category | flops | bytes accessed | tf_op | source)
XLA Modules:
  0.0 38.0 jit_solution(1789639404742371203)
XLA Ops:
  0.6 34.2 %shard_map.176 = (bf16[64,64,128]{2,1,0:T(8,128)(2,1)}, bf16[64,4096]{1,0:T(8,128)(2,1)}) custom-call(bf16[64,64,128]{2,1,0:T(8,128)(2,1)} %pair_hbm.1, s32[1,256]{1,0:T(1,128)} %bitcast.8, bf16[32,128]{1,0:T(8,128)(2,1)} %first_table_hbm.1, bf16[32,128]{1,0:T(8,128)(2,1)} %second_table_hbm.1, bf16[64,512]{1,0:T(8,128)(2,1)} %state_hbm.1, s32[16,64]{1,0:T(8,128)} %bitcast.7, ...), custom_call_target="tpu_custom_call" | custom-call | tf_op jit(solution)/shard_map/pallas_call | solution.py:644
  34.9 0.0 copy-start
  34.9 2.3 %copy.21 = bf16[64,64,128]{2,1,0:T(8,128)(2,1)} copy(bf16[64,64,128]{2,1,0:T(8,128)(2,1)} %get-tuple-element.4) | data formatting | bytes 2097152
  37.2 0.0 copy-done
  37.2 0.8 %copy.22 = bf16[64,4096]{1,0:T(8,128)(2,1)} copy(bf16[64,4096]{1,0:T(8,128)(2,1)S(1)} %copy-done) | data formatting | bytes 1048576
Async XLA Ops:
  34.9 2.3 %copy-start = (bf16[64,4096]{1,0:T(8,128)(2,1)S(1)}, bf16[64,4096]{1,0:T(8,128)(2,1)}, u32[]{:S(2)}) copy-start(bf16[64,4096]{1,0:T(8,128)(2,1)} %get-tuple-element.5) | copy-start | bytes 1572868

commit v2 on v1

--- a/solution.py
+++ b/solution.py
@@ -9,6 +9,10 @@
 
 EPSILON = 1e-05
 LANES = 128
+STORES = 4
+LAG = 3
+STRAIGHT = 1
+BATCH = 2
 MESH = pl.DeviceIdType.MESH
 
 
@@ -244,15 +248,32 @@
     def _():
         pl.semaphore_wait(barrier, 2 * (ranks - 1))
 
-    def left_copy(peer, slot):
+    chips = ranks // 2
+    partner = col + 1 - 2 * lax.rem(col, 2)
+
+    def across(step):
+        return lax.rem(col + 2 * step, ranks)
+
+    def left_copy(source_ref, peer, slot, place):
         return pltpu.make_async_remote_copy(
-            src_ref=left_ref,
+            src_ref=source_ref,
             dst_ref=left_all.at[pl.ds(slot * local_groups, local_groups)],
-            send_sem=left_send_sem.at[peer],
+            send_sem=left_send_sem.at[place],
             recv_sem=left_recv_sem.at[slot],
             device_id=(conf, row, peer),
             device_id_type=MESH,
         )
+
+    def left_forward(step):
+        slot = across(step)
+        return left_copy(
+            left_all.at[pl.ds(slot * local_groups, local_groups)], partner, slot, chips - 1 + step
+        )
+
+    left_sends = [left_copy(left_ref, across(step), col, step) for step in range(1, chips)]
+    left_sends.append(left_copy(left_ref, partner, col, 0))
+    for copy in left_sends:
+        copy.start()
 
     def right_copy(target, slot):
         return pltpu.make_async_remote_copy(
@@ -270,9 +291,6 @@
         @pl.when(jnp.logical_or(jnp.logical_not(diagonal), target != row))
         def _():
             right_copy(target, col).start()
-
-    for step in range(1, ranks):
-        left_copy(lax.rem(col + step, ranks), col).start()
 
     left_all[pl.ds(col * local_groups, local_groups)] = left_ref[...]
 
@@ -311,9 +329,11 @@
     for copy in last_loads:
         copy.wait()
 
-    for step in range(1, ranks):
-        peer = lax.rem(col + step, ranks)
-        left_copy(peer, peer).wait_recv()
+    for step in range(1, chips):
+        left_copy(left_ref, partner, across(step), 0).wait_recv()
+        left_forward(step).start()
+    for step in range(chips):
+        left_copy(left_ref, partner, lax.rem(partner + 2 * step, ranks), 0).wait_recv()
     for step in range(ranks):
         source = lax.rem(col + step, ranks)
 
@@ -335,7 +355,11 @@
             return jnp.concatenate(found, axis=0)
         return jnp.concatenate([part.astype(jnp.float32) for part in found], axis=0).astype(jnp.bfloat16)
 
-    def outer(group):
+    def outer(step):
+        for part in range(BATCH):
+            outer_group(step * BATCH + part, part * pairs)
+
+    def outer_group(group, offset):
         found = [
             left_all[group, :, tile * LANES : (tile + 1) * LANES].astype(jnp.float32)
             for tile in range(span_tiles)
@@ -367,14 +391,11 @@
             ).astype(jnp.bfloat16)
             for member in range(2):
                 for place in range(spans):
-                    outer_ref[
-                        (first + member) * block : (first + member + 1) * block,
-                        place * wide : (place + 1) * wide,
-                    ] = product[
+                    below = offset + (first + member) * block
+                    outer_ref[below : below + block, place * wide : (place + 1) * wide] = product[
                         place * block : (place + 1) * block, member * wide : (member + 1) * wide
                     ]
 
-    chips = ranks // 2
     far = (col // 2 == lax.rem(row // 2 + chips // 2, chips)) if chips > 1 else None
     relay = (col // 2 == row // 2) if chips > 1 else None
     relay_col = row // 2 * 2 + lax.rem(col, 2)
@@ -420,12 +441,13 @@
             mirror_copy(chunk, 0).start()
 
         if chips > 1:
-
-            @pl.when(far)
+            routed = jnp.logical_and(far, chunk < chunks - STRAIGHT)
+
+            @pl.when(routed)
             def _():
                 relay_copy(chunk, relay_col).start()
 
-            @pl.when(jnp.logical_not(jnp.logical_or(diagonal, far)))
+            @pl.when(jnp.logical_not(jnp.logical_or(diagonal, routed)))
             def _():
                 mirror_copy(chunk, 1).start()
         else:
@@ -439,7 +461,9 @@
         forward_copy(chunk).start()
 
     mask_rows, mask_cols = mask_ref.shape
-    groups_per_mask = groups // mask_rows
+    batch_members = BATCH * members
+    steps = groups // BATCH
+    steps_per_mask = steps // mask_rows
     mask_side = block // mask_cols
     tiles = block // 2 // chunks
     channels = pair_ref.shape[2]
@@ -447,28 +471,28 @@
     def project():
         return jnp.dot(outer_ref[...], outer_weight_ref[...], preferred_element_type=jnp.float32)
 
-    def normalise(group, summed):
+    def normalise(step, summed):
         update = summed * (1.0 / depth) + outer_bias_ref[...].astype(jnp.float32)
         mask_col = jnp.concatenate(
             [
                 jnp.full(
                     (mask_side, channels),
-                    mask_ref[group // groups_per_mask, place].astype(jnp.float32),
+                    mask_ref[step // steps_per_mask, place].astype(jnp.float32),
                     jnp.float32,
                 )
                 for place in range(mask_cols)
             ],
             axis=0,
         )
-        first = pl.multiple_of(group * members, members)
-        state = pair_ref[pl.ds(first, members)].astype(jnp.float32)
-        left_embed = left_embed_ref[pl.ds(first, members), :]
+        first = pl.multiple_of(step * batch_members, batch_members)
+        state = pair_ref[pl.ds(first, batch_members)].astype(jnp.float32)
+        left_embed = left_embed_ref[pl.ds(first, batch_members), :]
         start = (
             state
             + left_embed[:, None, :]
             + right_embed_ref[...][None]
-            + mask_col[None] * update.reshape(members, block, channels)
-        ).reshape(pairs, channels)
+            + mask_col[None] * update.reshape(batch_members, block, channels)
+        ).reshape(BATCH * pairs, channels)
         mean = jnp.mean(start, axis=-1, keepdims=True)
         centered = start - mean
         variance = jnp.mean(centered * centered, axis=-1, keepdims=True)
@@ -493,51 +517,51 @@
     def contract(start, hidden):
         branch = jnp.dot(hidden, down_ref[...], preferred_element_type=jnp.float32)
         result = (start + branch).astype(jnp.bfloat16)
-        shaped = result.reshape(members // 2, 2, block, channels)
+        shaped = result.reshape(batch_members // 2, 2, block, channels)
         joined = jnp.concatenate([shaped[:, 0], shaped[:, 1]], axis=-1).reshape(
-            members // 2 * block, 2 * channels
+            batch_members // 2 * block, 2 * channels
         )
         part = lax.dot_general(
             joined, dist_weight_wide[...], (((1,), (1,)), ((), ())),
             preferred_element_type=jnp.float32,
         )
-        return result, part.astype(jnp.bfloat16).reshape(members // 2, block, LANES)
-
-    last = groups - 1
+        return result, part.astype(jnp.bfloat16).reshape(batch_members // 2, block, LANES)
+
+    last = steps - 1
     outer(0)
     start_ref[...], normed_ref[...] = normalise(0, project())
     outer(1)
 
-    def group_step(group, carry):
+    def group_step(step, carry):
         start = start_ref[...]
         hidden = expand(normed_ref[...])
         summed = project()
         result, part = contract(start, hidden)
-        next_start, next_normed = normalise(jnp.minimum(group + 1, last), summed)
-        outer(jnp.minimum(group + 2, last))
-        first = pl.multiple_of(group * members, members)
-        pair_out_ref[pl.ds(first, members)] = result.reshape(members, block, channels)
+        next_start, next_normed = normalise(jnp.minimum(step + 1, last), summed)
+        outer(jnp.minimum(step + 2, last))
+        first = pl.multiple_of(step * batch_members, batch_members)
+        pair_out_ref[pl.ds(first, batch_members)] = result.reshape(batch_members, block, channels)
         wide = result.astype(jnp.float32)
-        for member in range(members):
+        for member in range(batch_members):
             pair_float[pl.ds((first + member) * pitch, block), :] = wide[
                 member * block : (member + 1) * block
             ]
-        mirror_send[pl.ds(group * (members // 2), members // 2)] = part
+        mirror_send[pl.ds(step * (batch_members // 2), batch_members // 2)] = part
         start_ref[...] = next_start
         normed_ref[...] = next_normed
         return carry
 
-    groups_per_chunk = groups // chunks
+    steps_per_chunk = steps // chunks
 
     def chunk_step(chunk, carry):
-        lax.fori_loop(chunk * groups_per_chunk, (chunk + 1) * groups_per_chunk, group_step, 0)
+        lax.fori_loop(chunk * steps_per_chunk, (chunk + 1) * steps_per_chunk, group_step, 0)
 
         send_chunk(chunk)
         if chips > 1:
 
-            @pl.when(jnp.logical_and(relay, chunk > 0))
+            @pl.when(jnp.logical_and(relay, chunk >= LAG))
             def _():
-                pass_on(chunk - 1)
+                pass_on(chunk - LAG)
 
         return carry
 
@@ -547,7 +571,8 @@
 
         @pl.when(relay)
         def _():
-            pass_on(chunks - 1)
+            for chunk in range(chunks - LAG, chunks - STRAIGHT):
+                pass_on(chunk)
 
     def own_step(tile, carry):
         even = pair_float[pl.ds(2 * tile, block, stride=pitch), :]
@@ -594,7 +619,7 @@
 
         @pl.when(relay)
         def _():
-            for chunk in range(chunks):
+            for chunk in range(chunks - STRAIGHT):
                 forward_copy(chunk).wait_send()
 
     for step in range(ranks):
@@ -604,8 +629,25 @@
         def _():
             right_copy(target, col).wait_send()
 
-    for step in range(1, ranks):
-        left_copy(lax.rem(col + step, ranks), col).wait_send()
+    for copy in left_sends:
+        copy.wait_send()
+    for step in range(1, chips):
+        left_forward(step).wait_send()
+
+
+def store(pair_ref, dist_ref, pair_hbm, dist_hbm, store_sem):
+    copies = []
+    for place, (source, target) in enumerate(((pair_ref, pair_hbm), (dist_ref, dist_hbm))):
+        rows = source.shape[0] // STORES
+        for part in range(STORES):
+            span = pl.ds(part * rows, rows)
+            copies.append(
+                pltpu.make_async_copy(source.at[span], target.at[span], store_sem.at[place, part])
+            )
+    for copy in copies:
+        copy.start()
+    for copy in copies:
+        copy.wait()
 
 
 def local(
@@ -637,15 +679,15 @@
     members = 2 * LANES // depth
     groups = block // members
     local_groups = local_tokens // members
-    chunks = block // 8
+    chunks = block // (BATCH * members)
 
     vmem = pl.BlockSpec(memory_space=pltpu.VMEM)
     hbm = pl.BlockSpec(memory_space=pltpu.HBM)
     pair_out, distogram = pl.pallas_call(
         functools.partial(kernel, ranks, depth, chunks),
         out_shape=(
-            jax.ShapeDtypeStruct(pair_state.shape, jnp.bfloat16),
-            jax.ShapeDtypeStruct((block, block * bins), jnp.bfloat16),
+            pltpu.VMEM(pair_state.shape, jnp.bfloat16),
+            pltpu.VMEM((block, block * bins), jnp.bfloat16),
         ),
         in_specs=[hbm] * 17,
         out_specs=(vmem, vmem),
@@ -654,7 +696,7 @@
             pltpu.VMEM((local_tokens, width * depth), jnp.bfloat16),
             pltpu.VMEM((groups, width, members * depth), jnp.bfloat16),
             pltpu.VMEM((ranks, local_tokens, width * depth), jnp.bfloat16),
-            pltpu.VMEM((members * block, width * width), jnp.bfloat16),
+            pltpu.VMEM((BATCH * members * block, width * width), jnp.bfloat16),
             pltpu.VMEM(outer_product_weight.shape, jnp.bfloat16),
             pltpu.VMEM(outer_product_weight.shape, jnp.float32),
             pltpu.VMEM(outer_product_weight.shape, jnp.bfloat16),
@@ -664,8 +706,8 @@
             pltpu.VMEM((block // 2, block, 2 * bins), jnp.bfloat16),
             pltpu.VMEM((block // 2, block, 2 * bins), jnp.bfloat16),
             pltpu.VMEM((block // 2, block, 2 * bins), jnp.float32),
-            pltpu.VMEM((members * block, channels), jnp.float32),
-            pltpu.VMEM((members * block, channels), jnp.bfloat16),
+            pltpu.VMEM((BATCH * members * block, channels), jnp.float32),
+            pltpu.VMEM((BATCH * members * block, channels), jnp.bfloat16),
             pltpu.SemaphoreType.DMA((ranks,)),
             pltpu.SemaphoreType.DMA((ranks,)),
             pltpu.SemaphoreType.DMA((ranks,)),
@@ -697,7 +739,9 @@
             pltpu.SemaphoreType.DMA((17,)),
         ],
         compiler_params=pltpu.CompilerParams(
-            collective_id=0, has_side_effects=True, vmem_limit_bytes=60 * 1024 * 1024
+            collective_id=0,
+            has_side_effects=True,
+            vmem_limit_bytes=56 * 1024 * 1024,
         ),
     )(
         pair_state,
@@ -718,7 +762,19 @@
         distance_weight.T,
         distance_bias[None],
     )
-    return pair_out, distogram
+    return pl.pallas_call(
+        store,
+        out_shape=(
+            jax.ShapeDtypeStruct(pair_state.shape, jnp.bfloat16),
+            jax.ShapeDtypeStruct((block, block * bins), jnp.bfloat16),
+        ),
+        in_specs=[vmem, vmem],
+        out_specs=(hbm, hbm),
+        scratch_shapes=[pltpu.SemaphoreType.DMA((2, STORES))],
+    )(
+        pltpu.with_memory_space_constraint(pair_out, pltpu.VMEM),
+        pltpu.with_memory_space_constraint(distogram, pltpu.VMEM),
+    )
 
 
 def solution(mesh):

time: 38.2 us -> 31.6 us (0.83)
  the two profiles are of different devices: /device:TPU:7 before, /device:TPU:1 now
where the time goes in v2:
time: 31.6 us; the launch traced here: 31.4 us
  Pallas kernels  30.7 us (97%)
  between operations  0.65 us (2%)
    pallas_call x1, Pallas kernels, local(): pl.pallas_call(functools.partial(kernel, ranks, depth, chunks), out_shape...  29.5 us
    pallas_call x1, Pallas kernels, local(): pl.pallas_call(store, out_shape=(jax.ShapeDtypeStruct(pair_state.shape, j...  1.2 us

profile of v2, /device:TPU:1, one launch (start us, length us, event | category | flops | bytes accessed | tf_op | source)
XLA Modules:
  0.0 31.4 jit_solution(14466114235892720202)
XLA Ops:
  0.6 29.5 %shard_map.176 = (bf16[64,64,128]{2,1,0:T(8,128)(2,1)S(1)}, bf16[64,4096]{1,0:T(8,128)(2,1)S(1)}) custom-call(bf16[64,64,128]{2,1,0:T(8,128)(2,1)} %pair_hbm.1, s32[1,256]{1,0:T(1,128)} %bitcast.8, bf16[32,128]{1,0:T(8,128)(2,1)} %first_table_hbm.1, bf16[32,128]{1,0:T(8,128)(2,1)} %second_table_hbm.1, bf16[64,512]{1,0:T(8,128)(2,1)} %state_hbm.1, ...), custom_call_target="tpu_custom_call" | custom-call | tf_op jit(solution)/shard_map/pallas_call | solution.py:686
  30.2 1.2 %shard_map.177 = (bf16[64,64,128]{2,1,0:T(8,128)(2,1)}, bf16[64,4096]{1,0:T(8,128)(2,1)}) custom-call(bf16[64,64,128]{2,1,0:T(8,128)(2,1)S(1)} %get-tuple-element.4.pair_ref, bf16[64,4096]{1,0:T(8,128)(2,1)S(1)} %get-tuple-element.5.dist_ref), custom_call_target="tpu_custom_call" | custom-call | tf_op jit(solution)/shard_map/pallas_call | solution.py:765

commit v3 on v2

--- a/solution.py
+++ b/solution.py
@@ -286,7 +286,7 @@
         )
 
     for step in range(ranks):
-        target = lax.rem(row + step, ranks)
+        target = jnp.where(row < ranks // 2, ranks - 1 - step, step)
 
         @pl.when(jnp.logical_or(jnp.logical_not(diagonal), target != row))
         def _():

time: 31.6 us -> 31.3 us (level)
  the two profiles are of different devices: /device:TPU:1 before, /device:TPU:2 now
where the time goes in v3:
time: 31.3 us; the launch traced here: 31.1 us
  Pallas kernels  30.4 us (97%)
  between operations  0.65 us (2%)
    pallas_call x1, Pallas kernels, local(): pl.pallas_call(functools.partial(kernel, ranks, depth, chunks), out_shape...  29.2 us
    pallas_call x1, Pallas kernels, local(): pl.pallas_call(store, out_shape=(jax.ShapeDtypeStruct(pair_state.shape, j...  1.2 us

profile of v3, /device:TPU:2, one launch (start us, length us, event | category | flops | bytes accessed | tf_op | source)
XLA Modules:
  0.0 31.1 jit_solution(17213068465723664178)
XLA Ops:
  0.6 29.2 %shard_map.176 = (bf16[64,64,128]{2,1,0:T(8,128)(2,1)S(1)}, bf16[64,4096]{1,0:T(8,128)(2,1)S(1)}) custom-call(bf16[64,64,128]{2,1,0:T(8,128)(2,1)} %pair_hbm.1, s32[1,256]{1,0:T(1,128)} %bitcast.8, bf16[32,128]{1,0:T(8,128)(2,1)} %first_table_hbm.1, bf16[32,128]{1,0:T(8,128)(2,1)} %second_table_hbm.1, bf16[64,512]{1,0:T(8,128)(2,1)} %state_hbm.1, ...), custom_call_target="tpu_custom_call" | custom-call | tf_op jit(solution)/shard_map/pallas_call | solution.py:686
  29.9 1.2 %shard_map.177 = (bf16[64,64,128]{2,1,0:T(8,128)(2,1)}, bf16[64,4096]{1,0:T(8,128)(2,1)}) custom-call(bf16[64,64,128]{2,1,0:T(8,128)(2,1)S(1)} %get-tuple-element.4.pair_ref, bf16[64,4096]{1,0:T(8,128)(2,1)S(1)} %get-tuple-element.5.dist_ref), custom_call_target="tpu_custom_call" | custom-call | tf_op jit(solution)/shard_map/pallas_call | solution.py:765
